TPU v7x, 128 devices: a whole 4x4x4 slice. The times are simulated.
128 devices in a mesh: dp: 16 (over z, x), member: 8 (over y, core).
Axes of the slice: x: 4, y: 4, z: 4, core: 2. Of those that a mesh axis runs over, the one named last changes fastest.
Arguments:
- fixed_rows: bfloat16 [131072, 2048], P(('dp', 'member')), may hold values from -600 to 600
- member_rows: bfloat16 [131072, 256], P(('dp', 'member')), may hold values from -0.375 to 0.375
- target: float32 [131072], P(('dp', 'member')), may hold values from -6 to 6
- fixed_prev: bfloat16 [2048], replicated, may hold values from -0.59765625 to 0.59765625
- member_id: int32 [131072], P(('dp', 'member')), may hold values from 0 to 511, as said below
Outputs:
- fixed_coef: float32 [2048], replicated
- member_coef: float32 [512, 256], P(('dp', 'member'))
- row_scores: float32 [131072], P(('dp', 'member'))
Inputs may be any that keep to these rules, and one draw needn't show every extreme that they name: `member_id`: member m belongs to owner m // 4, the device of that index along dp+member, which holds its row of member_coef. Among the 1024 rows of one device (aligned blocks) at most 24 have members of one owner; in every draw one owner gets exactly 24 rows from every device.
All inputs are finite; a program needn't handle non-finite values.
Results may differ from a plain program's by a relative error of at most 0.006.
Values may be sent and summed in bfloat16 or wider, within the bound.
No kernel may reach another device: no remote copies, remote signals or barrier semaphores. Data moves between devices by JAX's collectives and lax.ppermute only.
A program may use at most 192 MiB of HBM per device.

v0:
```python
import functools

import jax
import jax.numpy as jnp
from jax import lax
from jax.experimental import pallas as pl
from jax.experimental.pallas import tpu as pltpu
from jax.sharding import Mesh
from jax.sharding import PartitionSpec as P

F32 = jnp.float32
BF16 = jnp.bfloat16
HIGH = lax.Precision.HIGHEST
ALL = ("z", "x", "y", "core")
CHIPS = ("z", "x", "y")

MEM_DEV = 4
RIDGE_FIXED = 4.0
RIDGE_MEMBER = 1.0

FIX = 2048
MEM = 256
PAY = 384
BLK = 256
NBLK = FIX // BLK
CORE_PAIRS = 18


def pair_table():
    table = []
    for core in range(2):
        pairs = []
        for i in range(4 * core, 4 * core + 4):
            pairs += [(i, (i + k) % NBLK) for k in range(4)]
        pairs += [(0, 4), (1, 5)] if core == 0 else [(6, 2), (7, 3)]
        table.append(sorted((max(p), min(p)) for p in pairs))
    return table


def params(mb=56):
    return pltpu.CompilerParams(vmem_limit_bytes=mb << 20)


def dot_nn(a, b, precision=None):
    return lax.dot_general(a, b, (((1,), (0,)), ((), ())), precision=precision, preferred_element_type=F32)


def dot_nt(a, b, precision=None):
    return lax.dot_general(a, b, (((1,), (1,)), ((), ())), precision=precision, preferred_element_type=F32)


def dot_tn(a, b, precision=None):
    return lax.dot_general(a, b, (((0,), (0,)), ((), ())), precision=precision, preferred_element_type=F32)


def cost(us):
    return pl.CostEstimate(flops=int(us * 1e9), transcendentals=0, bytes_accessed=int(us * 2e6))


def split3(v):
    hi = v.astype(BF16)
    rest = v - hi.astype(F32)
    mid = rest.astype(BF16)
    low = (rest - mid.astype(F32)).astype(BF16)
    return hi, mid, low


def as_left(v, axis):
    h, m, l = split3(v)
    return jnp.concatenate([h, h, m, h, l, m], axis=axis)


def as_right(v, axis):
    h, m, l = split3(v)
    return jnp.concatenate([h, m, h, l, h, m], axis=axis)


def full_nn(a, b):
    return dot_nn(as_left(a, 1), as_right(b, 0))


def full_nt(a, b):
    return dot_nt(as_left(a, 1), as_right(b, 1))


def over_lanes(v, c):
    return jnp.broadcast_to(v[:, c : c + 1], v.shape)


def over_rows(v, i):
    return jnp.broadcast_to(v[i : i + 1, :], v.shape)


def factor128(blocks, aside=None):
    n = len(blocks)
    sub = lax.broadcasted_iota(jnp.int32, (8, 128), 0)
    lane = lax.broadcasted_iota(jnp.int32, (8, 128), 1)
    a = [[blk[8 * t : 8 * t + 8, :] for t in range(16)] for blk in blocks]
    e = [[(lane == sub + 8 * t).astype(F32) for t in range(16)] for _ in blocks]
    out = [[] for _ in blocks]
    b = [[over_lanes(a[p][0], k) for k in range(8)] for p in range(n)]
    for s in range(16):
        more = s < 15
        if aside is not None:
            aside(s)
        r = [a[p][s] for p in range(n)]
        f = [e[p][s] for p in range(n)]
        if more:
            r1 = [a[p][s + 1] for p in range(n)]
            f1 = [e[p][s + 1] for p in range(n)]
            q = [[over_lanes(r1[p], 8 * s + k) for k in range(8)] for p in range(n)]
            bn = [[over_lanes(r1[p], 8 * s + 8 + k) for k in range(8)] for p in range(n)]
        scale = [jnp.zeros((8, 128), F32) for _ in range(n)]
        for i in range(8):
            for p in range(n):
                inv = 1.0 / over_rows(b[p][i], i)
                scale[p] = jnp.where(sub == i, inv, scale[p])
                ri, fi = over_rows(r[p], i), over_rows(f[p], i)
                if i < 7:
                    m = jnp.where(sub > i, b[p][i] * inv, 0.0)
                    r[p] = r[p] - m * ri
                    f[p] = f[p] - m * fi
                bk = [None] * 8
                for k in range(i + 1, 8):
                    bk[k] = over_rows(b[p][k], i)
                    b[p][k] = b[p][k] - m * bk[k]
                if more:
                    mq = q[p][i] * inv
                    r1[p] = r1[p] - mq * ri
                    f1[p] = f1[p] - mq * fi
                    for k in range(i + 1, 8):
                        q[p][k] = q[p][k] - mq * bk[k]
                    for k in range(8):
                        bn[p][k] = bn[p][k] - mq * over_rows(q[p][i], k)
        for p in range(n):
            root = jnp.sqrt(scale[p])
            y, z = r[p] * root, f[p] * root
            out[p].append(z)
            if more:
                a[p][s + 1], e[p][s + 1] = r1[p], f1[p]
                b[p] = bn[p]
            if s < 14:
                both = jnp.concatenate([y, z], axis=1)
                u = dot_tn(as_left(y, 0), as_right(both, 0))
                for t in range(s + 2, 16):
                    a[p][t] = a[p][t] - u[8 * t : 8 * t + 8, :128]
                    e[p][t] = e[p][t] - u[8 * t : 8 * t + 8, 128:]
    return [jnp.concatenate(o, axis=0) for o in out]


def dispatch_kernel(cap, fix_ref, prev_ref, target_ref, id_ref, rows_ref, send_ref, slot_ref):
    count = rows_ref.shape[0]
    owners = send_ref.shape[0] // cap
    prior = dot_nt(prev_ref[...], fix_ref[...])
    resid = (target_ref[...] - prior).astype(BF16)
    ids = id_ref[...]
    owner = ids // MEM_DEV
    local = ids - owner * MEM_DEV
    hot = lax.broadcasted_iota(jnp.int32, (owners, count), 0) == owner
    before = (
        lax.broadcasted_iota(jnp.int32, (count, count), 0)
        < lax.broadcasted_iota(jnp.int32, (count, count), 1)
    ).astype(BF16)
    ahead = dot_nn(hot.astype(BF16), before)
    place = jnp.sum(jnp.where(hot, ahead, 0.0), axis=0, keepdims=True)
    slot = owner * cap + place.astype(jnp.int32)
    slot_ref[...] = slot
    kind = lax.broadcasted_iota(jnp.int32, (128, count), 0)
    meta = jnp.where(
        kind == 0,
        jnp.broadcast_to(resid.astype(F32), (128, count)),
        (kind == local + 1).astype(F32),
    ).astype(BF16)
    rows = rows_ref[...]

    def place_rows(c, carry):
        pick = (
            lax.broadcasted_iota(jnp.int32, (256, count), 0) + 256 * c == slot
        ).astype(BF16)
        at = pl.ds(pl.multiple_of(256 * c, 256), 256)
        send_ref[at, :MEM] = dot_nn(pick, rows).astype(BF16)
        send_ref[at, MEM:] = dot_nt(pick, meta).astype(BF16)
        return carry

    lax.fori_loop(0, owners * cap // 256, place_rows, 0)


def member_kernel(recv_ref, coef_ref, score_ref, turned_ref, gram_ref, rhs_ref):
    slots = recv_ref.shape[0]
    unit = (
        lax.broadcasted_iota(jnp.int32, (PAY, PAY), 0)
        == lax.broadcasted_iota(jnp.int32, (PAY, PAY), 1)
    ).astype(BF16)

    def turn(c, carry):
        at = pl.ds(pl.multiple_of(256 * c, 256), 256)
        turned_ref[:, at] = dot_nt(unit, recv_ref[at, :]).astype(BF16)
        return carry

    lax.fori_loop(0, slots // 256, turn, 0)
    rows = recv_ref[:, :MEM]
    hots = turned_ref[MEM + 1 : MEM + 1 + MEM_DEV, :]
    resid = turned_ref[MEM : MEM + 1, :]
    rhs_ref[...] = dot_nn(hots * resid, rows)
    ridge = jnp.where(
        lax.broadcasted_iota(jnp.int32, (MEM, MEM), 0)
        == lax.broadcasted_iota(jnp.int32, (MEM, MEM), 1),
        RIDGE_MEMBER,
        0.0,
    )
    for m in range(MEM_DEV):
        gram_ref[m] = ridge

    def collect(c, carry):
        at = pl.ds(pl.multiple_of(512 * c, 512), 512)
        piece = turned_ref[:MEM, at]
        hot = turned_ref[MEM + 1 : MEM + 1 + MEM_DEV, at]
        tall = jnp.concatenate([piece * hot[m : m + 1] for m in range(MEM_DEV)], axis=0)
        gain = dot_nn(tall, recv_ref[at, :MEM])
        for m in range(MEM_DEV):
            gram_ref[m] = gram_ref[m] + gain[MEM * m : MEM * m + MEM]
        return carry

    lax.fori_loop(0, slots // 512, collect, 0)

    grams = [gram_ref[m] for m in range(MEM_DEV)]
    w0 = factor128([g[:128, :128] for g in grams])
    l10 = [full_nt(g[128:, :128], w) for g, w in zip(grams, w0)]
    w1 = factor128([g[128:, 128:] - full_nt(l, l) for g, l in zip(grams, l10)])
    for m in range(MEM_DEV):
        right = rhs_ref[m : m + 1, :]
        y0 = full_nt(right[:, :128], w0[m])
        y1 = full_nt(right[:, 128:] - full_nt(y0, l10[m]), w1[m])
        x1 = full_nn(y1, w1[m])
        x0 = full_nn(y0 - full_nn(x1, l10[m]), w0[m])
        coef_ref[m : m + 1, :] = jnp.concatenate([x0, x1], axis=1)
    low = coef_ref[...].astype(BF16)
    projected = dot_nn(low, turned_ref[:MEM, :])
    score_ref[...] = jnp.sum(projected * hots.astype(F32), axis=0, keepdims=True)


def combine_kernel(back_ref, slot_ref, target_ref, score_ref, resid_ref):
    slots, count = back_ref.shape[1], slot_ref.shape[1]
    parts = split3(back_ref[...])
    stack = jnp.concatenate([part.astype(F32) for part in parts] + [jnp.zeros((5, slots), F32)], axis=0).astype(BF16)
    slot = slot_ref[...]
    total = jnp.zeros((8, count), F32)
    for c in range(slots // 256):
        pick = (
            lax.broadcasted_iota(jnp.int32, (256, count), 0) + 256 * c == slot
        ).astype(BF16)
        total = total + dot_nn(stack[:, 256 * c : 256 * c + 256], pick)
    score = total[0:1] + (total[1:2] + total[2:3])
    score_ref[...] = score
    resid_ref[...] = (target_ref[...] - score).astype(BF16)


def gram_kernel(hi_ref, lo_ref, own_ref, other_ref, out_ref, turned_ref):
    rows = own_ref.shape[0]
    unit = (
        lax.broadcasted_iota(jnp.int32, (BLK, BLK), 0)
        == lax.broadcasted_iota(jnp.int32, (BLK, BLK), 1)
    ).astype(BF16)

    def turn(i, carry):
        lanes = pl.ds(pl.multiple_of(BLK * i, BLK), BLK)
        turned_ref[i, :, :rows] = dot_nt(unit, own_ref[:, lanes]).astype(BF16)
        turned_ref[i, :, rows:] = dot_nt(unit, other_ref[:, lanes]).astype(BF16)
        return carry

    lax.fori_loop(0, NBLK, turn, 0)

    def block(b, carry):
        left = turned_ref[hi_ref[b]]
        lanes = pl.ds(pl.multiple_of(lo_ref[b] * BLK, BLK), BLK)
        value = dot_nn(left[:, :rows], own_ref[:, lanes]) + dot_nn(left[:, rows:], other_ref[:, lanes])
        out_ref[:32, b] = value[:, :128].reshape(32, 8, 128)
        out_ref[32:, b] = value[:, 128:].reshape(32, 8, 128)
        return carry

    lax.fori_loop(0, CORE_PAIRS, block, 0)


def gram_blocks(own, other, hi, lo):
    rows = own.shape[0]
    return pl.pallas_call(
        gram_kernel,
        out_shape=jax.ShapeDtypeStruct((64, CORE_PAIRS, 8, 128), F32),
        in_specs=[pl.BlockSpec(memory_space=pltpu.SMEM)] * 2
        + [pl.BlockSpec(memory_space=pltpu.VMEM)] * 2,
        out_specs=pl.BlockSpec(memory_space=pltpu.VMEM),
        scratch_shapes=[pltpu.VMEM((NBLK, BLK, 2 * rows), BF16)],
        compiler_params=params(28),
        name="gram",
        cost_estimate=cost(10),
    )(hi, lo, own, other)


def place_of(i, j):
    return i * (i + 1) // 2 + j


def read_block(a_ref, at):
    flat = a_ref[at].reshape(2 * BLK, 128)
    return jnp.concatenate([flat[:BLK], flat[BLK:]], axis=1)


def write_block(a_ref, at, value):
    a_ref[at] = jnp.concatenate([value[:, :128], value[:, 128:]], axis=0).reshape(64, 8, 128)


WIDE = 32
SLIM = 16


def job_table():
    spare = NBLK * (NBLK + 1) // 2
    table = []
    for k in range(NBLK):
        jobs = []
        if k:
            jobs = [(i, j, place_of(i, j)) for i in range(k, NBLK) for j in range(k, i + 1)][1:]
        jobs += [(NBLK - 1, NBLK - 1, spare)] * (WIDE - len(jobs))
        table.append([entry for job in jobs for entry in job])
    return table


def factor_kernel(table_ref, gram_ref, a_ref, w_ref, done_ref, left_ref, right_ref, sems):
    copies = []
    for core, pairs in enumerate(pair_table()):
        for b, (i, j) in enumerate(pairs):
            at = place_of(i, j)
            copies.append(
                pltpu.make_async_copy(gram_ref.at[:, core, b], a_ref.at[at], sems.at[at])
            )
    for copy in copies:
        copy.start()
    for copy in copies:
        copy.wait()
    left_ref[NBLK - 1] = jnp.zeros((BLK, 6 * BLK), BF16)
    right_ref[NBLK - 1] = jnp.zeros((BLK, 6 * BLK), BF16)
    a_ref[NBLK * (NBLK + 1) // 2] = jnp.zeros((64, 8, 128), F32)
    ridge = jnp.where(
        lax.broadcasted_iota(jnp.int32, (128, 128), 0)
        == lax.broadcasted_iota(jnp.int32, (128, 128), 1),
        RIDGE_FIXED,
        0.0,
    )

    def trail(i, j, at):
        gain = dot_nt(left_ref[i], right_ref[j])
        flat = jnp.concatenate([gain[:, :128], gain[:, 128:]], axis=0)
        a_ref[at] = a_ref[at] - flat.reshape(64, 8, 128)

    def diagonal(k, every):
        def aside(first):
            def emit(s):
                if s % every == 0:
                    slot = 3 * (first + s // every)
                    trail(table_ref[k, slot], table_ref[k, slot + 1], table_ref[k, slot + 2])

            return emit

        diag = a_ref[place_of(k, k)].reshape(2 * BLK, 128)
        w00 = factor128([diag[:128] + ridge], aside(0))[0]
        l10 = full_nt(diag[128:256], w00)
        cross = full_nn(l10, w00)
        w11 = factor128([diag[384:] + ridge - full_nt(l10, l10)], aside(16 // every))[0]
        w_ref[k, :128, :128] = w00
        w_ref[k, :128, 128:] = jnp.zeros((128, 128), F32)
        w_ref[k, 128:, :128] = -full_nn(w11, cross)
        w_ref[k, 128:, 128:] = w11

    def step(k, carry):
        wide = (k == 1) | (k == 2)

        @pl.when(wide)
        def _():
            diagonal(k, 1)

        @pl.when(jnp.logical_not(wide))
        def _():
            diagonal(k, 2)

        whole = as_right(w_ref[k], 1)

        def panel(i, carry):
            at = place_of(i, k)
            value = dot_nt(as_left(read_block(a_ref, at), 1), whole)
            write_block(a_ref, at, value)
            h, m, l = split3(value)
            left_ref[i] = jnp.concatenate([h, h, m, h, l, m], axis=1)
            right_ref[i] = jnp.concatenate([h, m, h, l, h, m], axis=1)
            return carry

        lax.fori_loop(k + 1, NBLK, panel, 0)

        @pl.when(k + 1 < NBLK)
        def _():
            trail(k + 1, k + 1, place_of(k + 1, k + 1))

        return carry

    lax.fori_loop(0, NBLK, step, 0)
    done_ref[...] = jnp.zeros((8, 128), F32)


def factor_fixed(gram):
    count = NBLK * (NBLK + 1) // 2
    return pl.pallas_call(
        factor_kernel,
        out_shape=(
            jax.ShapeDtypeStruct((count + 1, 64, 8, 128), F32),
            jax.ShapeDtypeStruct((NBLK, BLK, BLK), F32),
            jax.ShapeDtypeStruct((8, 128), F32),
        ),
        in_specs=[pl.BlockSpec(memory_space=pltpu.SMEM), pl.BlockSpec(memory_space=pl.ANY)],
        out_specs=(
            pl.BlockSpec(memory_space=pltpu.VMEM),
            pl.BlockSpec(memory_space=pltpu.VMEM),
            pl.BlockSpec(memory_space=pltpu.VMEM),
        ),
        scratch_shapes=[
            pltpu.VMEM((NBLK, BLK, 6 * BLK), BF16),
            pltpu.VMEM((NBLK, BLK, 6 * BLK), BF16),
            pltpu.SemaphoreType.DMA((count,)),
        ],
        compiler_params=params(46),
        name="factor_fixed",
        cost_estimate=cost(100),
    )(jnp.array(job_table(), jnp.int32), gram)


def halves(a_ref, at):
    flat = a_ref[at].reshape(2 * BLK, 128)
    return flat[:BLK], flat[BLK:]


def solve_kernel(low_ref, w_ref, grad_ref, fix_ref, member_ref, coef_ref, score_ref, a_ref, sems):
    copies = {}
    for k in range(1, NBLK):
        for j in range(k):
            at = place_of(k, j)
            copies[k, j] = pltpu.make_async_copy(low_ref.at[at], a_ref.at[at], sems.at[at])
            copies[k, j].start()
    turned = [w_ref[k].T for k in range(NBLK)]

    def times_row(left, right, row):
        return left * row[:, :128] + right * row[:, 128:]

    def as_column(spread):
        return jnp.sum(spread, axis=1, keepdims=True)

    forward = []
    for k in range(NBLK):
        part = grad_ref[:, BLK * k : BLK * k + BLK].T
        if k:
            total = jnp.zeros((BLK, 128), F32)
            for j in range(k):
                copies[k, j].wait()
                left, right = halves(a_ref, place_of(k, j))
                total = total + times_row(left, right, forward[j])
            part = part - as_column(total)
        forward.append(jnp.sum(turned[k] * part, axis=0, keepdims=True))
    backward = [None] * NBLK
    for k in range(NBLK - 1, -1, -1):
        part = forward[k]
        if k + 1 < NBLK:
            total = [jnp.zeros((8, 128), F32) for _ in range(2)]
            for i in range(k + 1, NBLK):
                for h, piece in enumerate(halves(a_ref, place_of(i, k))):
                    gain = (piece * backward[i]).reshape(BLK // 8, 8, 128)
                    total[h] = total[h] + jnp.sum(gain, axis=0)
            part = part - jnp.concatenate(
                [jnp.sum(total[h], axis=0, keepdims=True) for h in range(2)], axis=1
            )
        backward[k] = as_column(times_row(turned[k][:, :128], turned[k][:, 128:], part))
    coef = jnp.concatenate([jnp.broadcast_to(x, (BLK, 128)).T[:1] for x in backward], axis=1)
    coef_ref[...] = coef
    score_ref[...] = dot_nt(coef.astype(BF16), fix_ref[...]) + member_ref[...]


def shards(fixed_rows, member_rows, target, fixed_prev, member_id):
    count = fixed_rows.shape[0]
    devices = lax.axis_size(ALL)
    cap = 3 * count // devices
    slots = devices * cap
    core = lax.axis_index("core")
    swap = [(0, 1), (1, 0)]
    other = lax.ppermute(fixed_rows, "core", swap)

    target_row = target.reshape(1, count)
    send, slot = pl.pallas_call(
        functools.partial(dispatch_kernel, cap),
        out_shape=(
            jax.ShapeDtypeStruct((slots, PAY), BF16),
            jax.ShapeDtypeStruct((1, count), jnp.int32),
        ),
        compiler_params=params(),
        name="dispatch",
        cost_estimate=cost(9),
    )(fixed_rows, fixed_prev.reshape(1, FIX), target_row, member_id.reshape(1, count), member_rows)
    other, send = lax.optimization_barrier((other, send))

    table = jnp.array(pair_table(), jnp.int32)[core]
    gram = gram_blocks(fixed_rows, other, table[:, 0], table[:, 1])
    shares = lax.all_to_all(gram, CHIPS, split_axis=0, concat_axis=0, tiled=True)
    shares, send = lax.optimization_barrier((shares, send))
    recv = lax.all_to_all(send.reshape(devices, cap, PAY), ALL, split_axis=0, concat_axis=0, tiled=True)
    share = jnp.sum(shares, axis=0)
    whole = lax.all_gather(share, ALL, axis=0, tiled=False)
    whole = whole.reshape(devices // 2, 2, CORE_PAIRS, 8, 128)

    member_coef, slot_score = pl.pallas_call(
        member_kernel,
        out_shape=(
            jax.ShapeDtypeStruct((MEM_DEV, MEM), F32),
            jax.ShapeDtypeStruct((1, slots), F32),
        ),
        scratch_shapes=[
            pltpu.VMEM((PAY, slots), BF16),
            pltpu.VMEM((MEM_DEV, MEM, MEM), F32),
            pltpu.VMEM((MEM_DEV, MEM), F32),
        ],
        compiler_params=params(),
        name="members",
        cost_estimate=cost(30),
    )(recv.reshape(slots, PAY))
    back = lax.all_to_all(slot_score.reshape(devices, cap), ALL, split_axis=0, concat_axis=0, tiled=True)
    member_score, fixed_resid = pl.pallas_call(
        combine_kernel,
        out_shape=(
            jax.ShapeDtypeStruct((1, count), F32),
            jax.ShapeDtypeStruct((1, count), BF16),
        ),
        compiler_params=params(),
        name="combine",
        cost_estimate=cost(3),
    )(back.reshape(1, slots), slot, target_row)
    gradient = dot_nn(fixed_resid, fixed_rows)
    spread = jnp.broadcast_to(gradient[None], (devices, 1, FIX))
    gradients = lax.all_to_all(spread, ALL, split_axis=0, concat_axis=0, tiled=True)

    lower, inverses, done = factor_fixed(whole)
    gradients, done = lax.optimization_barrier((gradients, done))
    gradient = jnp.sum(gradients, axis=0) + done[:1, :1]
    count_blocks = NBLK * (NBLK + 1) // 2
    near = pl.BlockSpec(memory_space=pltpu.VMEM)
    fixed_coef, row_scores = pl.pallas_call(
        solve_kernel,
        out_shape=(
            jax.ShapeDtypeStruct((1, FIX), F32),
            jax.ShapeDtypeStruct((1, count), F32),
        ),
        in_specs=[pl.BlockSpec(memory_space=pl.ANY), near, near, near, near],
        out_specs=(near, near),
        scratch_shapes=[
            pltpu.VMEM((count_blocks, 64, 8, 128), F32),
            pltpu.SemaphoreType.DMA((count_blocks,)),
        ],
        compiler_params=params(48),
        name="substitute",
        cost_estimate=cost(12),
    )(lower, inverses, gradient, fixed_rows, member_score)
    return (fixed_coef.reshape(FIX), member_coef, row_scores.reshape(count))


def solution(mesh):
    grid = Mesh(mesh.devices.reshape(4, 4, 4, 2), ALL)
    placed = (P(ALL, None), P(ALL, None), P(ALL), P(), P(ALL))
    return jax.shard_map(
        shards,
        mesh=grid,
        in_specs=placed,
        out_specs=(P(), P(ALL, None), P(ALL)),
        check_vma=False,
    )
```

profile of v0, /device:TPU:1, one launch (start us, length us, event | category | flops | bytes accessed | tf_op | source)
XLA Modules:
  0.0 322.1 jit_solution(5268864632757550837)
XLA Ops:
  7.2 0.0 all-gather.3.cloned.1.call-start
  7.2 1.5 collective-permute-start
  8.7 1.3 reshape.59.prev_ref
  10.0 0.7 dynamic-slice_bitcast_fusion
  10.7 0.0 copy-start
  10.7 10.9 %dispatch.1 = (bf16[3072,384]{1,0:T(8,128)(2,1)}, s32[1,1024]{1,0:T(1,128)}) custom-call(bf16[1024,2048]{1,0:T(8,128)(2,1)} %fix_ref.3, bf16[1,2048]{1,0:T(2,128)(2,1)} %reshape.59.prev_ref, f32[1,1024]{1,0:T(1,128)} %bitcast.28, s32[1,1024]{1,0:T(1,128)} %bitcast.27, bf16[1024,256]{1,0:T(8,128)(2,1)} %rows_ref.1), custom_call_target="tpu_custom_call" | custom-call | flops 8999999488 | bytes 18000000 | tf_op jit(solution)/shard_map/dispatch/pallas_call | solution.py:493
  21.6 0.0 collective-permute-done.other_ref
  21.6 0.0 copy-done
  21.6 14.4 %gram.1 = f32[64,18,8,128]{3,2,1,0:T(8,128)S(1)} custom-call(s32[18]{0:T(128)S(1)} %get-tuple-element.38.hi_ref, s32[18]{0:T(128)S(1)} %get-tuple-element.37.lo_ref, bf16[1024,2048]{1,0:T(8,128)(2,1)S(1)} %copy-done, bf16[1024,2048]{1,0:T(8,128)(2,1)} %collective-permute-done.other_ref), custom_call_target="tpu_custom_call" | custom-call | flops 10000000000 | bytes 20000000 | tf_op jit(solution)/shard_map/gram/pallas_call | solution.py:286
  36.0 68.7 %all_to_all.24 = f32[64,18,8,128]{3,2,1,0:T(8,128)} all-to-all(f32[64,18,8,128]{3,2,1,0:T(8,128)S(1)} %gram.1), channel_id=1, replica_groups=mesh['z'=4,'x'=4,'y'=4,'core'=2] {'z','x','y'}, dimensions={0} | all-to-all | bytes 9437184 | tf_op jit(solution)/shard_map/all_to_all | solution.py:507
  104.8 0.0 copy-start.4
  104.8 3.3 %reduce_sum.18 = f32[18,8,128]{2,1,0:T(8,128)} reduce(f32[64,18,8,128]{3,2,1,0:T(8,128)} %all_to_all.24, f32[]{:T(128)} %constant.5.clone.1), dimensions={0}, to_apply=%region_0.0 | reduce | flops 1161216 | bytes 4792324 | tf_op jit(solution)/shard_map/reduce_sum | solution.py:510
  108.1 0.0 all-gather.3.cloned.1.call-update
  108.2 0.0 copy-done.4
  108.2 39.8 %all_to_all.25 = bf16[128,24,384]{2,1,0:T(8,128)(2,1)} all-to-all(bf16[128,24,384]{2,1,0:T(8,128)(2,1)S(1)} %bitcast.22), channel_id=1, replica_groups=mesh['z'=4,'x'=4,'y'=4,'core'=2] {'z','x','y','core'}, dimensions={0} | all-to-all | bytes 4718592 | tf_op jit(solution)/shard_map/all_to_all | solution.py:509
  148.0 39.4 %members.1 = (f32[4,256]{1,0:T(4,128)}, f32[1,3072]{1,0:T(1,128)}) custom-call(bf16[3072,384]{1,0:T(8,128)(2,1)} %bitcast.23), custom_call_target="tpu_custom_call" | custom-call | flops 30000001024 | bytes 60000000 | tf_op jit(solution)/shard_map/members/pallas_call | solution.py:514
  187.4 0.5 broadcast.19
  187.9 1.4 reduce.7
  189.3 0.1 all_to_all.17
  189.4 13.5 %all_to_all.26 = f32[128,1,24]{2,1,0:T(1,128)S(1)} all-to-all(f32[128,1,24]{2,1,0:T(1,128)S(1)} %bitcast.24), channel_id=1, replica_groups=mesh['z'=4,'x'=4,'y'=4,'core'=2] {'z','x','y','core'}, dimensions={0} | all-to-all | bytes 24576 | tf_op jit(solution)/shard_map/all_to_all | solution.py:529
  202.9 0.8 reduce.8
  203.7 0.7 reshape.65.back_ref
  204.4 0.0 copy-start.1
  204.4 2.5 combine.1
  206.9 0.0 copy-start.2
  206.9 0.0 copy-done.1
  206.9 1.3 fusion
  208.3 1.5 broadcast_in_dim.2
  209.8 4.4 %all-to-all-start.3 = ((f32[128,1,2048]{2,1,0:T(1,128)}), f32[128,1,2048]{2,1,0:T(1,128)S(1)}, u32[]{:S(2)}, u32[]{:S(2)}) async-start(f32[128,1,2048]{2,1,0:T(1,128)} %broadcast_in_dim.2), calls=%async_computation.3 | async-start | bytes 2097152 | tf_op jit(solution)/shard_map/all_to_all | solution.py:542
  214.2 0.0 all-gather.3.cloned.1.call-done
  214.2 0.0 copy-done.2
  214.2 0.0 copy-start.3
  214.3 90.0 %factor_fixed.1 = (f32[37,64,8,128]{3,2,1,0:T(8,128)}, f32[8,256,256]{2,1,0:T(8,128)S(1)}, f32[8,128]{1,0:T(8,128)S(1)}) custom-call(s32[8,96]{1,0:T(8,128)S(1)} %copy-done.2, f32[64,2,18,8,128]{4,3,2,1,0:T(8,128)} %bitcast.26), custom_call_target="tpu_custom_call" | custom-call | flops 99999997952 | bytes 200000000 | tf_op jit(solution)/shard_map/factor_fixed/pallas_call | solution.py:410
  304.3 0.0 all-to-all-done.3
  304.3 0.5 slice.11
  304.8 0.6 reduce_sum.19
  305.4 0.6 broadcast_add_fusion
  306.1 0.0 copy-done.3
  306.1 8.9 %substitute.1 = (f32[1,2048]{1,0:T(1,128)}, f32[1,1024]{1,0:T(1,128)}) custom-call(f32[37,64,8,128]{3,2,1,0:T(8,128)} %get-tuple-element.24.low_ref, f32[8,256,256]{2,1,0:T(8,128)S(1)} %get-tuple-element.25.w_ref, f32[1,2048]{1,0:T(1,128)S(1)} %bitcast.21, bf16[1024,2048]{1,0:T(8,128)(2,1)} %fix_ref.3, f32[1,1024]{1,0:T(1,128)S(1)} %copy-done.3), custom_call_target="tpu_custom_call" | custom-call | flops 12000000000 | bytes 24000000 | tf_op jit(solution)/shard_map/substitute/pallas_call | solution.py:549
  (1 shorter events, 0.0 us)
Async XLA Ops:
  7.2 207.1 %all-gather.3.cloned.1.call-start = ((), (), s32[]{:S(2)}) async-start(), calls=%async_computation.4 | async-start | bytes 9510912 | tf_op jit(solution)/shard_map/all_gather | solution.py:511
  7.2 14.4 %collective-permute-start = (bf16[1024,2048]{1,0:T(8,128)(2,1)}, bf16[1024,2048]{1,0:T(8,128)(2,1)}, u32[]{:S(2)}, u32[]{:S(2)}) collective-permute-start(bf16[1024,2048]{1,0:T(8,128)(2,1)} %fix_ref.3), channel_id=1, source_target_pairs={{0,1},{1,0},{2,3},{3,2},{4,5},{5,4},{6,7},{7,6},{8,9},{9,8},{10,11... | collective-permute-start | bytes 12582920 | tf_op jit(solution)/shard_map/ppermute | solution.py:490
  10.7 10.9 %copy-start = (bf16[1024,2048]{1,0:T(8,128)(2,1)S(1)}, bf16[1024,2048]{1,0:T(8,128)(2,1)}, u32[]{:S(2)}) copy-start(bf16[1024,2048]{1,0:T(8,128)(2,1)} %fix_ref.3) | copy-start | bytes 12582916
  104.8 3.4 %copy-start.4 = (bf16[3072,384]{1,0:T(8,128)(2,1)S(1)}, bf16[3072,384]{1,0:T(8,128)(2,1)}, u32[]{:S(2)}) copy-start(bf16[3072,384]{1,0:T(8,128)(2,1)} %get-tuple-element.26) | copy-start | bytes 7077892
  204.4 2.5 copy-start.1
  206.9 7.3 %copy-start.2 = (s32[8,96]{1,0:T(8,128)S(1)}, s32[8,96]{1,0:T(8,128)}, u32[]{:S(2)}) copy-start(s32[8,96]{1,0:T(8,128)} %constant.15.clone.table_ref) | copy-start | bytes 9220
  209.8 94.5 %all-to-all-start.3 = ((f32[128,1,2048]{2,1,0:T(1,128)}), f32[128,1,2048]{2,1,0:T(1,128)S(1)}, u32[]{:S(2)}, u32[]{:S(2)}) async-start(f32[128,1,2048]{2,1,0:T(1,128)} %broadcast_in_dim.2), calls=%async_computation.3 | async-start | bytes 2097152 | tf_op jit(solution)/shard_map/all_to_all | solution.py:542
  214.2 91.9 %copy-start.3 = (f32[1,1024]{1,0:T(1,128)S(1)}, f32[1,1024]{1,0:T(1,128)}, u32[]{:S(2)}) copy-start(f32[1,1024]{1,0:T(1,128)} %get-tuple-element.33.member_ref) | copy-start | bytes 12292
Sparse Core Ops, SparseCore 0:
  108.3 82.8 all-gather.2
where the time goes:
time: 321 us; the launch traced here: 322 us
  Pallas kernels  166 us (52%)
  blocking collectives  122 us (38%)
  between operations  14.4 us (4%)
  other arithmetic  6.82 us (2%)
  starting transfers between devices  5.94 us (2%)
  local copies, waits for them, and re-layouts  5.33 us (2%)
    pallas_call x1, Pallas kernels, factor_fixed(): pl.pallas_call(factor_kernel, out_shape=(jax.ShapeDtypeStruct((count + 1,...  90 us
    all_to_all x1, blocking collectives, shards(): lax.all_to_all(gram, CHIPS, split_axis=0, concat_axis=0, tiled=True)  68.7 us
    all_to_all x1, blocking collectives, shards(): lax.all_to_all(send.reshape(devices, cap, PAY), ALL, split_axis=0, concat...  39.8 us
    pallas_call x1, Pallas kernels, shards(): pl.pallas_call(member_kernel, out_shape=(jax.ShapeDtypeStruct((MEM_DEV, M...  39.4 us
    pallas_call x1, Pallas kernels, gram_blocks(): pl.pallas_call(gram_kernel, out_shape=jax.ShapeDtypeStruct((64, CORE_PAIR...  14.4 us
    all_to_all x1, blocking collectives, shards(): lax.all_to_all(slot_score.reshape(devices, cap), ALL, split_axis=0, conca...  13.5 us
    pallas_call x1, Pallas kernels, shards(): pl.pallas_call(functools.partial(dispatch_kernel, cap), out_shape=(jax.Sh...  10.9 us
    pallas_call x1, Pallas kernels, shards(): pl.pallas_call(solve_kernel, out_shape=(jax.ShapeDtypeStruct((1, FIX), F3...  8.91 us
  transfers between devices with their start and end apart: 3, of which 0 were waited for; matrix products, arithmetic and copies ran while one was open for 3% of the time, Pallas kernels for 44%

commit v1 on v0

--- a/solution.py
+++ b/solution.py
@@ -209,19 +209,7 @@
         0.0,
     )
     for m in range(MEM_DEV):
-        gram_ref[m] = ridge
-
-    def collect(c, carry):
-        at = pl.ds(pl.multiple_of(512 * c, 512), 512)
-        piece = turned_ref[:MEM, at]
-        hot = turned_ref[MEM + 1 : MEM + 1 + MEM_DEV, at]
-        tall = jnp.concatenate([piece * hot[m : m + 1] for m in range(MEM_DEV)], axis=0)
-        gain = dot_nn(tall, recv_ref[at, :MEM])
-        for m in range(MEM_DEV):
-            gram_ref[m] = gram_ref[m] + gain[MEM * m : MEM * m + MEM]
-        return carry
-
-    lax.fori_loop(0, slots // 512, collect, 0)
+        gram_ref[m] = dot_nn(turned_ref[:MEM, :] * hots[m : m + 1, :], rows) + ridge
 
     grams = [gram_ref[m] for m in range(MEM_DEV)]
     w0 = factor128([g[:128, :128] for g in grams])
@@ -261,14 +249,11 @@
         lax.broadcasted_iota(jnp.int32, (BLK, BLK), 0)
         == lax.broadcasted_iota(jnp.int32, (BLK, BLK), 1)
     ).astype(BF16)
-
-    def turn(i, carry):
-        lanes = pl.ds(pl.multiple_of(BLK * i, BLK), BLK)
-        turned_ref[i, :, :rows] = dot_nt(unit, own_ref[:, lanes]).astype(BF16)
-        turned_ref[i, :, rows:] = dot_nt(unit, other_ref[:, lanes]).astype(BF16)
-        return carry
-
-    lax.fori_loop(0, NBLK, turn, 0)
+    for part, ref in enumerate((own_ref, other_ref)):
+        for i in range(NBLK):
+            turned_ref[i, :, rows * part : rows * part + rows] = dot_nt(
+                unit, ref[:, BLK * i : BLK * i + BLK]
+            ).astype(BF16)
 
     def block(b, carry):
         left = turned_ref[hi_ref[b]]
@@ -290,7 +275,7 @@
         + [pl.BlockSpec(memory_space=pltpu.VMEM)] * 2,
         out_specs=pl.BlockSpec(memory_space=pltpu.VMEM),
         scratch_shapes=[pltpu.VMEM((NBLK, BLK, 2 * rows), BF16)],
-        compiler_params=params(28),
+        compiler_params=params(56),
         name="gram",
         cost_estimate=cost(10),
     )(hi, lo, own, other)
@@ -333,10 +318,11 @@
             copies.append(
                 pltpu.make_async_copy(gram_ref.at[:, core, b], a_ref.at[at], sems.at[at])
             )
+    first = pair_table()[0].index((0, 0))
+    copies = [copies[first]] + copies[:first] + copies[first + 1 :]
     for copy in copies:
         copy.start()
-    for copy in copies:
-        copy.wait()
+    copies[0].wait()
     left_ref[NBLK - 1] = jnp.zeros((BLK, 6 * BLK), BF16)
     right_ref[NBLK - 1] = jnp.zeros((BLK, 6 * BLK), BF16)
     a_ref[NBLK * (NBLK + 1) // 2] = jnp.zeros((64, 8, 128), F32)
@@ -381,6 +367,11 @@
         @pl.when(jnp.logical_not(wide))
         def _():
             diagonal(k, 2)
+
+        @pl.when(k == 0)
+        def _():
+            for copy in copies[1:]:
+                copy.wait()
 
         whole = as_right(w_ref[k], 1)
 
@@ -436,13 +427,15 @@
     return flat[:BLK], flat[BLK:]
 
 
-def solve_kernel(low_ref, w_ref, grad_ref, fix_ref, member_ref, coef_ref, score_ref, a_ref, sems):
+def solve_kernel(low_ref, w_ref, grad_ref, far_ref, member_ref, coef_ref, score_ref, a_ref, fix_ref, sems, fix_sem):
     copies = {}
     for k in range(1, NBLK):
         for j in range(k):
             at = place_of(k, j)
             copies[k, j] = pltpu.make_async_copy(low_ref.at[at], a_ref.at[at], sems.at[at])
             copies[k, j].start()
+    fix_copy = pltpu.make_async_copy(far_ref, fix_ref, fix_sem)
+    fix_copy.start()
     turned = [w_ref[k].T for k in range(NBLK)]
 
     def times_row(left, right, row):
@@ -477,6 +470,7 @@
         backward[k] = as_column(times_row(turned[k][:, :128], turned[k][:, 128:], part))
     coef = jnp.concatenate([jnp.broadcast_to(x, (BLK, 128)).T[:1] for x in backward], axis=1)
     coef_ref[...] = coef
+    fix_copy.wait()
     score_ref[...] = dot_nt(coef.astype(BF16), fix_ref[...]) + member_ref[...]
 
 
@@ -489,7 +483,11 @@
     swap = [(0, 1), (1, 0)]
     other = lax.ppermute(fixed_rows, "core", swap)
 
+    table = jnp.array(pair_table(), jnp.int32)[core]
+    gram = gram_blocks(fixed_rows, other, table[:, 0], table[:, 1])
     target_row = target.reshape(1, count)
+    gram, ids = lax.optimization_barrier((gram, member_id.reshape(1, count)))
+    shares = lax.all_to_all(gram, CHIPS, split_axis=0, concat_axis=0, tiled=True)
     send, slot = pl.pallas_call(
         functools.partial(dispatch_kernel, cap),
         out_shape=(
@@ -499,12 +497,7 @@
         compiler_params=params(),
         name="dispatch",
         cost_estimate=cost(9),
-    )(fixed_rows, fixed_prev.reshape(1, FIX), target_row, member_id.reshape(1, count), member_rows)
-    other, send = lax.optimization_barrier((other, send))
-
-    table = jnp.array(pair_table(), jnp.int32)[core]
-    gram = gram_blocks(fixed_rows, other, table[:, 0], table[:, 1])
-    shares = lax.all_to_all(gram, CHIPS, split_axis=0, concat_axis=0, tiled=True)
+    )(fixed_rows, fixed_prev.reshape(1, FIX), target_row, ids, member_rows)
     shares, send = lax.optimization_barrier((shares, send))
     recv = lax.all_to_all(send.reshape(devices, cap, PAY), ALL, split_axis=0, concat_axis=0, tiled=True)
     share = jnp.sum(shares, axis=0)
@@ -552,11 +545,13 @@
             jax.ShapeDtypeStruct((1, FIX), F32),
             jax.ShapeDtypeStruct((1, count), F32),
         ),
-        in_specs=[pl.BlockSpec(memory_space=pl.ANY), near, near, near, near],
+        in_specs=[pl.BlockSpec(memory_space=pl.ANY), near, near, pl.BlockSpec(memory_space=pl.ANY), near],
         out_specs=(near, near),
         scratch_shapes=[
             pltpu.VMEM((count_blocks, 64, 8, 128), F32),
+            pltpu.VMEM((count, FIX), BF16),
             pltpu.SemaphoreType.DMA((count_blocks,)),
+            pltpu.SemaphoreType.DMA,
         ],
         compiler_params=params(48),
         name="substitute",

time: 321 us -> 316 us (0.984)
  blocking collectives: 122 us -> 56.4 us
  waiting for transfers between devices: 0.04 us -> 54.1 us
  starting transfers between devices: 5.94 us -> 17.5 us
  Pallas kernels: 166 us -> 162 us
    all_to_all x1 -> x0, blocking collectives: 68.7 us -> none  [shards(): lax.all_to_all(gram, CHIPS, split_axis=0, concat_axis=0, tiled=True)]
    all_to_all x0 -> x1, waiting for transfers between devices: none -> 48.1 us  [shards(): lax.all_to_all(gram, CHIPS, split_axis=0, concat_axis=0, tiled=True)]
    all_to_all x0 -> x1, starting transfers between devices: none -> 11.6 us  [shards(): lax.all_to_all(gram, CHIPS, split_axis=0, concat_axis=0, tiled=True)]
    ppermute x1, waiting for transfers between devices: 0.01 us -> 5.93 us  [shards(): other = lax.ppermute(fixed_rows, 'core', swap)]
  transfers between devices with their start and end apart: 3 -> 4, of which waited for: 0 -> 2; matrix products, arithmetic and copies ran while one was open for 3% -> 3% of each run, Pallas kernels for 44% -> 44%
where the time goes in v1:
time: 316 us; the launch traced here: 317 us
  Pallas kernels  162 us (51%)
  blocking collectives  56.4 us (18%)
  waiting for transfers between devices  54.1 us (17%)
  starting transfers between devices  17.5 us (6%)
  between operations  14.4 us (5%)
  other arithmetic  6.69 us (2%)
  local copies, waits for them, and re-layouts  5.14 us (2%)
    pallas_call x1, Pallas kernels, factor_fixed(): pl.pallas_call(factor_kernel, out_shape=(jax.ShapeDtypeStruct((count + 1,...  87.3 us
    all_to_all x1, waiting for transfers between devices, shards(): lax.all_to_all(gram, CHIPS, split_axis=0, concat_axis=0, tiled=True)  48.1 us
    all_to_all x1, blocking collectives, shards(): lax.all_to_all(send.reshape(devices, cap, PAY), ALL, split_axis=0, concat...  42.9 us
    pallas_call x1, Pallas kernels, shards(): pl.pallas_call(member_kernel, out_shape=(jax.ShapeDtypeStruct((MEM_DEV, M...  37.9 us
    pallas_call x1, Pallas kernels, gram_blocks(): pl.pallas_call(gram_kernel, out_shape=jax.ShapeDtypeStruct((64, CORE_PAIR...  16.4 us
    all_to_all x1, blocking collectives, shards(): lax.all_to_all(slot_score.reshape(devices, cap), ALL, split_axis=0, conca...  13.5 us
    all_to_all x1, starting transfers between devices, shards(): lax.all_to_all(gram, CHIPS, split_axis=0, concat_axis=0, tiled=True)  11.6 us
    pallas_call x1, Pallas kernels, shards(): pl.pallas_call(functools.partial(dispatch_kernel, cap), out_shape=(jax.Sh...  10.7 us
  transfers between devices with their start and end apart: 4, of which 2 were waited for; matrix products, arithmetic and copies ran while one was open for 3% of the time, Pallas kernels for 44%

profile of v1, /device:TPU:1, one launch (start us, length us, event | category | flops | bytes accessed | tf_op | source)
XLA Modules:
  0.0 317.4 jit_solution(11963935376899931279)
XLA Ops:
  7.2 1.5 collective-permute-start
  8.7 0.7 dynamic-slice_bitcast_fusion
  9.3 0.5 slice_bitcast_fusion
  9.9 5.9 %collective-permute-done.other_ref = bf16[1024,2048]{1,0:T(8,128)(2,1)} collective-permute-done((bf16[1024,2048]{1,0:T(8,128)(2,1)}, bf16[1024,2048]{1,0:T(8,128)(2,1)}, u32[]{:S(2)}, u32[]{:S(2)}) %collective-permute-start) | collective-permute-done | bytes 4194336 | tf_op jit(solution)/shard_map/ppermute | solution.py:484
  15.8 16.4 %gram.1 = f32[64,18,8,128]{3,2,1,0:T(8,128)} custom-call(s32[18]{0:T(128)} %get-tuple-element.38.hi_ref, s32[18]{0:T(128)} %get-tuple-element.37.lo_ref, bf16[1024,2048]{1,0:T(8,128)(2,1)} %far_ref.1, bf16[1024,2048]{1,0:T(8,128)(2,1)} %collective-permute-done.other_ref), custom_call_target="tpu_custom_call" | custom-call | flops 10000000000 | bytes 20000000 | tf_op jit(solution)/shard_map/gram/pallas_call | solution.py:271
  32.2 0.0 copy-start.4
  32.2 11.6 %all-to-all-start = ((f32[64,18,8,128]{3,2,1,0:T(8,128)}), f32[64,18,8,128]{3,2,1,0:T(8,128)}, u32[]{:S(2)}, u32[]{:S(2)}) async-start(f32[64,18,8,128]{3,2,1,0:T(8,128)} %gram.1), calls=%async_computation | async-start | bytes 9437184 | tf_op jit(solution)/shard_map/all_to_all | solution.py:490
  43.8 0.0 all-gather.3.cloned.1.call-start
  43.9 0.0 copy-done.4
  43.9 0.6 reshape.60.prev_ref
  44.5 10.7 %dispatch.1 = (bf16[3072,384]{1,0:T(8,128)(2,1)}, s32[1,1024]{1,0:T(1,128)}) custom-call(bf16[1024,2048]{1,0:T(8,128)(2,1)} %far_ref.1, bf16[1,2048]{1,0:T(2,128)(2,1)} %reshape.60.prev_ref, f32[1,1024]{1,0:T(1,128)} %bitcast.28, s32[1,1024]{1,0:T(1,128)} %bitcast.27, bf16[1024,256]{1,0:T(8,128)(2,1)} %rows_ref.1), custom_call_target="tpu_custom_call" | custom-call | flops 8999999488 | bytes 18000000 | tf_op jit(solution)/shard_map/dispatch/pallas_call | solution.py:491
  55.2 0.0 copy-start.3
  55.2 48.1 %all-to-all-done = f32[64,18,8,128]{3,2,1,0:T(8,128)} async-done(((f32[64,18,8,128]{3,2,1,0:T(8,128)}), f32[64,18,8,128]{3,2,1,0:T(8,128)}, u32[]{:S(2)}, u32[]{:S(2)}) %all-to-all-start) | async-done | bytes 4718624 | tf_op jit(solution)/shard_map/all_to_all | solution.py:490
  103.3 3.2 %reduce_sum.18 = f32[18,8,128]{2,1,0:T(8,128)} reduce(f32[64,18,8,128]{3,2,1,0:T(8,128)} %all-to-all-done, f32[]{:T(128)} %constant.5.clone.1), dimensions={0}, to_apply=%region_0.0 | reduce | flops 1161216 | bytes 4792324 | tf_op jit(solution)/shard_map/reduce_sum | solution.py:503
  106.5 0.0 all-gather.3.cloned.1.call-update
  106.5 0.0 copy-done.3
  106.6 42.9 %all_to_all.24 = bf16[128,24,384]{2,1,0:T(8,128)(2,1)} all-to-all(bf16[128,24,384]{2,1,0:T(8,128)(2,1)S(1)} %bitcast.22), channel_id=1, replica_groups=mesh['z'=4,'x'=4,'y'=4,'core'=2] {'z','x','y','core'}, dimensions={0} | all-to-all | bytes 4718592 | tf_op jit(solution)/shard_map/all_to_all | solution.py:502
  149.4 37.9 %members.1 = (f32[4,256]{1,0:T(4,128)}, f32[1,3072]{1,0:T(1,128)}) custom-call(bf16[3072,384]{1,0:T(8,128)(2,1)} %bitcast.23), custom_call_target="tpu_custom_call" | custom-call | flops 30000001024 | bytes 60000000 | tf_op jit(solution)/shard_map/members/pallas_call | solution.py:507
  187.4 0.5 broadcast.19
  187.9 1.4 reduce.7
  189.3 0.1 all_to_all.17
  189.4 13.5 %all_to_all.25 = f32[128,1,24]{2,1,0:T(1,128)S(1)} all-to-all(f32[128,1,24]{2,1,0:T(1,128)S(1)} %bitcast.24), channel_id=1, replica_groups=mesh['z'=4,'x'=4,'y'=4,'core'=2] {'z','x','y','core'}, dimensions={0} | all-to-all | bytes 24576 | tf_op jit(solution)/shard_map/all_to_all | solution.py:522
  202.9 0.8 reduce.8
  203.7 0.7 reshape.65.back_ref
  204.4 0.0 copy-start.2
  204.4 2.5 combine.1
  206.9 0.0 copy-start
  206.9 0.0 copy-done.2
  206.9 1.3 fusion
  208.2 1.5 broadcast_in_dim.2
  209.7 4.4 %all-to-all-start.3 = ((f32[128,1,2048]{2,1,0:T(1,128)}), f32[128,1,2048]{2,1,0:T(1,128)S(1)}, u32[]{:S(2)}, u32[]{:S(2)}) async-start(f32[128,1,2048]{2,1,0:T(1,128)} %broadcast_in_dim.2), calls=%async_computation.3 | async-start | bytes 2097152 | tf_op jit(solution)/shard_map/all_to_all | solution.py:535
  214.1 0.0 all-gather.3.cloned.1.call-done
  214.2 0.0 copy-done
  214.2 0.0 copy-start.1
  214.2 87.3 %factor_fixed.1 = (f32[37,64,8,128]{3,2,1,0:T(8,128)}, f32[8,256,256]{2,1,0:T(8,128)S(1)}, f32[8,128]{1,0:T(8,128)S(1)}) custom-call(s32[8,96]{1,0:T(8,128)S(1)} %copy-done, f32[64,2,18,8,128]{4,3,2,1,0:T(8,128)} %bitcast.26), custom_call_target="tpu_custom_call" | custom-call | flops 99999997952 | bytes 200000000 | tf_op jit(solution)/shard_map/factor_fixed/pallas_call | solution.py:401
  301.5 0.0 all-to-all-done.3
  301.5 0.5 slice.11
  302.1 0.6 reduce_sum.19
  302.7 0.6 broadcast_add_fusion
  303.4 0.0 copy-done.1
  303.4 6.9 %substitute.1 = (f32[1,2048]{1,0:T(1,128)}, f32[1,1024]{1,0:T(1,128)}) custom-call(f32[37,64,8,128]{3,2,1,0:T(8,128)} %get-tuple-element.24.low_ref, f32[8,256,256]{2,1,0:T(8,128)S(1)} %get-tuple-element.25.w_ref, f32[1,2048]{1,0:T(1,128)S(1)} %bitcast.21, bf16[1024,2048]{1,0:T(8,128)(2,1)} %far_ref.1, f32[1,1024]{1,0:T(1,128)S(1)} %copy-done.1), custom_call_target="tpu_custom_call" | custom-call | flops 12000000000 | bytes 24000000 | tf_op jit(solution)/shard_map/substitute/pallas_call | solution.py:542
Async XLA Ops:
  7.2 8.6 %collective-permute-start = (bf16[1024,2048]{1,0:T(8,128)(2,1)}, bf16[1024,2048]{1,0:T(8,128)(2,1)}, u32[]{:S(2)}, u32[]{:S(2)}) collective-permute-start(bf16[1024,2048]{1,0:T(8,128)(2,1)} %far_ref.1), channel_id=1, source_target_pairs={{0,1},{1,0},{2,3},{3,2},{4,5},{5,4},{6,7},{7,6},{8,9},{9,8},{10,11... | collective-permute-start | bytes 12582920 | tf_op jit(solution)/shard_map/ppermute | solution.py:484
  32.2 11.7 %copy-start.4 = (bf16[2048]{0:T(1024)(128)(2,1)S(1)}, bf16[2048]{0:T(1024)(128)(2,1)}, u32[]{:S(2)}) copy-start(bf16[2048]{0:T(1024)(128)(2,1)} %param.10) | copy-start | bytes 12292
  32.2 71.1 %all-to-all-start = ((f32[64,18,8,128]{3,2,1,0:T(8,128)}), f32[64,18,8,128]{3,2,1,0:T(8,128)}, u32[]{:S(2)}, u32[]{:S(2)}) async-start(f32[64,18,8,128]{3,2,1,0:T(8,128)} %gram.1), calls=%async_computation | async-start | bytes 9437184 | tf_op jit(solution)/shard_map/all_to_all | solution.py:490
  43.8 170.3 %all-gather.3.cloned.1.call-start = ((), (), s32[]{:S(2)}) async-start(), calls=%async_computation.4 | async-start | bytes 9510912 | tf_op jit(solution)/shard_map/all_gather | solution.py:504
  55.2 51.3 %copy-start.3 = (bf16[3072,384]{1,0:T(8,128)(2,1)S(1)}, bf16[3072,384]{1,0:T(8,128)(2,1)}, u32[]{:S(2)}) copy-start(bf16[3072,384]{1,0:T(8,128)(2,1)} %get-tuple-element.26) | copy-start | bytes 7077892
  204.4 2.5 copy-start.2
  206.9 7.3 %copy-start = (s32[8,96]{1,0:T(8,128)S(1)}, s32[8,96]{1,0:T(8,128)}, u32[]{:S(2)}) copy-start(s32[8,96]{1,0:T(8,128)} %constant.15.clone.table_ref) | copy-start | bytes 9220
  209.7 91.8 %all-to-all-start.3 = ((f32[128,1,2048]{2,1,0:T(1,128)}), f32[128,1,2048]{2,1,0:T(1,128)S(1)}, u32[]{:S(2)}, u32[]{:S(2)}) async-start(f32[128,1,2048]{2,1,0:T(1,128)} %broadcast_in_dim.2), calls=%async_computation.3 | async-start | bytes 2097152 | tf_op jit(solution)/shard_map/all_to_all | solution.py:535
  214.2 89.2 %copy-start.1 = (f32[1,1024]{1,0:T(1,128)S(1)}, f32[1,1024]{1,0:T(1,128)}, u32[]{:S(2)}) copy-start(f32[1,1024]{1,0:T(1,128)} %get-tuple-element.33.member_ref) | copy-start | bytes 12292
Sparse Core Ops, SparseCore 0:
  106.7 85.9 all-gather.2

commit v2 on v1

--- a/solution.py
+++ b/solution.py
@@ -191,13 +191,10 @@
         lax.broadcasted_iota(jnp.int32, (PAY, PAY), 0)
         == lax.broadcasted_iota(jnp.int32, (PAY, PAY), 1)
     ).astype(BF16)
-
-    def turn(c, carry):
-        at = pl.ds(pl.multiple_of(256 * c, 256), 256)
-        turned_ref[:, at] = dot_nt(unit, recv_ref[at, :]).astype(BF16)
-        return carry
-
-    lax.fori_loop(0, slots // 256, turn, 0)
+    for c in range(slots // 256):
+        turned_ref[:, 256 * c : 256 * c + 256] = dot_nt(
+            unit, recv_ref[256 * c : 256 * c + 256, :]
+        ).astype(BF16)
     rows = recv_ref[:, :MEM]
     hots = turned_ref[MEM + 1 : MEM + 1 + MEM_DEV, :]
     resid = turned_ref[MEM : MEM + 1, :]

time: 316 us -> 314 us (level)
  transfers between devices with their start and end apart: 4 -> 4, of which waited for: 2 -> 2; matrix products, arithmetic and copies ran while one was open for 3% -> 3% of each run, Pallas kernels for 44% -> 43%
where the time goes in v2:
time: 314 us; the launch traced here: 315 us
  Pallas kernels  160 us (51%)
  blocking collectives  56.4 us (18%)
  waiting for transfers between devices  54.1 us (17%)
  starting transfers between devices  17.5 us (6%)
  between operations  14.4 us (5%)
  other arithmetic  6.67 us (2%)
  local copies, waits for them, and re-layouts  5.14 us (2%)
    pallas_call x1, Pallas kernels, factor_fixed(): pl.pallas_call(factor_kernel, out_shape=(jax.ShapeDtypeStruct((count + 1,...  87.3 us
    all_to_all x1, waiting for transfers between devices, shards(): lax.all_to_all(gram, CHIPS, split_axis=0, concat_axis=0, tiled=True)  48.1 us
    all_to_all x1, blocking collectives, shards(): lax.all_to_all(send.reshape(devices, cap, PAY), ALL, split_axis=0, concat...  42.9 us
    pallas_call x1, Pallas kernels, shards(): pl.pallas_call(member_kernel, out_shape=(jax.ShapeDtypeStruct((MEM_DEV, M...  35.8 us
    pallas_call x1, Pallas kernels, gram_blocks(): pl.pallas_call(gram_kernel, out_shape=jax.ShapeDtypeStruct((64, CORE_PAIR...  16.4 us
    all_to_all x1, blocking collectives, shards(): lax.all_to_all(slot_score.reshape(devices, cap), ALL, split_axis=0, conca...  13.5 us
    all_to_all x1, starting transfers between devices, shards(): lax.all_to_all(gram, CHIPS, split_axis=0, concat_axis=0, tiled=True)  11.6 us
    pallas_call x1, Pallas kernels, shards(): pl.pallas_call(functools.partial(dispatch_kernel, cap), out_shape=(jax.Sh...  10.7 us
  transfers between devices with their start and end apart: 4, of which 2 were waited for; matrix products, arithmetic and copies ran while one was open for 3% of the time, Pallas kernels for 43%

profile of v2, /device:TPU:1, one launch (start us, length us, event | category | flops | bytes accessed | tf_op | source)
XLA Modules:
  0.0 315.2 jit_solution(16674067900469195748)
XLA Ops:
  7.2 1.5 collective-permute-start
  8.7 0.7 dynamic-slice_bitcast_fusion
  9.3 0.5 slice_bitcast_fusion
  9.9 5.9 %collective-permute-done.other_ref = bf16[1024,2048]{1,0:T(8,128)(2,1)} collective-permute-done((bf16[1024,2048]{1,0:T(8,128)(2,1)}, bf16[1024,2048]{1,0:T(8,128)(2,1)}, u32[]{:S(2)}, u32[]{:S(2)}) %collective-permute-start) | collective-permute-done | bytes 4194336 | tf_op jit(solution)/shard_map/ppermute | solution.py:481
  15.8 16.4 %gram.1 = f32[64,18,8,128]{3,2,1,0:T(8,128)} custom-call(s32[18]{0:T(128)} %get-tuple-element.38.hi_ref, s32[18]{0:T(128)} %get-tuple-element.37.lo_ref, bf16[1024,2048]{1,0:T(8,128)(2,1)} %far_ref.1, bf16[1024,2048]{1,0:T(8,128)(2,1)} %collective-permute-done.other_ref), custom_call_target="tpu_custom_call" | custom-call | flops 10000000000 | bytes 20000000 | tf_op jit(solution)/shard_map/gram/pallas_call | solution.py:268
  32.2 0.0 copy-start.4
  32.2 11.6 %all-to-all-start = ((f32[64,18,8,128]{3,2,1,0:T(8,128)}), f32[64,18,8,128]{3,2,1,0:T(8,128)}, u32[]{:S(2)}, u32[]{:S(2)}) async-start(f32[64,18,8,128]{3,2,1,0:T(8,128)} %gram.1), calls=%async_computation | async-start | bytes 9437184 | tf_op jit(solution)/shard_map/all_to_all | solution.py:487
  43.8 0.0 all-gather.3.cloned.1.call-start
  43.9 0.0 copy-done.4
  43.9 0.6 reshape.60.prev_ref
  44.5 10.7 %dispatch.1 = (bf16[3072,384]{1,0:T(8,128)(2,1)}, s32[1,1024]{1,0:T(1,128)}) custom-call(bf16[1024,2048]{1,0:T(8,128)(2,1)} %far_ref.1, bf16[1,2048]{1,0:T(2,128)(2,1)} %reshape.60.prev_ref, f32[1,1024]{1,0:T(1,128)} %bitcast.28, s32[1,1024]{1,0:T(1,128)} %bitcast.27, bf16[1024,256]{1,0:T(8,128)(2,1)} %rows_ref.1), custom_call_target="tpu_custom_call" | custom-call | flops 8999999488 | bytes 18000000 | tf_op jit(solution)/shard_map/dispatch/pallas_call | solution.py:488
  55.2 0.0 copy-start.3
  55.2 48.1 %all-to-all-done = f32[64,18,8,128]{3,2,1,0:T(8,128)} async-done(((f32[64,18,8,128]{3,2,1,0:T(8,128)}), f32[64,18,8,128]{3,2,1,0:T(8,128)}, u32[]{:S(2)}, u32[]{:S(2)}) %all-to-all-start) | async-done | bytes 4718624 | tf_op jit(solution)/shard_map/all_to_all | solution.py:487
  103.3 3.2 %reduce_sum.18 = f32[18,8,128]{2,1,0:T(8,128)} reduce(f32[64,18,8,128]{3,2,1,0:T(8,128)} %all-to-all-done, f32[]{:T(128)} %constant.5.clone.1), dimensions={0}, to_apply=%region_0.0 | reduce | flops 1161216 | bytes 4792324 | tf_op jit(solution)/shard_map/reduce_sum | solution.py:500
  106.5 0.0 all-gather.3.cloned.1.call-update
  106.5 0.0 copy-done.3
  106.6 42.9 %all_to_all.24 = bf16[128,24,384]{2,1,0:T(8,128)(2,1)} all-to-all(bf16[128,24,384]{2,1,0:T(8,128)(2,1)S(1)} %bitcast.22), channel_id=1, replica_groups=mesh['z'=4,'x'=4,'y'=4,'core'=2] {'z','x','y','core'}, dimensions={0} | all-to-all | bytes 4718592 | tf_op jit(solution)/shard_map/all_to_all | solution.py:499
  149.4 35.8 %members.1 = (f32[4,256]{1,0:T(4,128)}, f32[1,3072]{1,0:T(1,128)}) custom-call(bf16[3072,384]{1,0:T(8,128)(2,1)} %bitcast.23), custom_call_target="tpu_custom_call" | custom-call | flops 30000001024 | bytes 60000000 | tf_op jit(solution)/shard_map/members/pallas_call | solution.py:504
  185.2 0.5 broadcast.19
  185.7 1.4 reduce.7
  187.1 0.1 all_to_all.17
  187.2 13.5 %all_to_all.25 = f32[128,1,24]{2,1,0:T(1,128)S(1)} all-to-all(f32[128,1,24]{2,1,0:T(1,128)S(1)} %bitcast.24), channel_id=1, replica_groups=mesh['z'=4,'x'=4,'y'=4,'core'=2] {'z','x','y','core'}, dimensions={0} | all-to-all | bytes 24576 | tf_op jit(solution)/shard_map/all_to_all | solution.py:519
  200.7 0.8 reduce.8
  201.5 0.7 reshape.65.back_ref
  202.2 0.0 copy-start.2
  202.2 2.5 combine.1
  204.7 0.0 copy-start
  204.7 0.0 copy-done.2
  204.7 1.3 fusion
  206.1 1.5 broadcast_in_dim.2
  207.6 4.4 %all-to-all-start.3 = ((f32[128,1,2048]{2,1,0:T(1,128)}), f32[128,1,2048]{2,1,0:T(1,128)S(1)}, u32[]{:S(2)}, u32[]{:S(2)}) async-start(f32[128,1,2048]{2,1,0:T(1,128)} %broadcast_in_dim.2), calls=%async_computation.3 | async-start | bytes 2097152 | tf_op jit(solution)/shard_map/all_to_all | solution.py:532
  212.0 0.0 all-gather.3.cloned.1.call-done
  212.0 0.0 copy-done
  212.0 0.0 copy-start.1
  212.0 87.3 %factor_fixed.1 = (f32[37,64,8,128]{3,2,1,0:T(8,128)}, f32[8,256,256]{2,1,0:T(8,128)S(1)}, f32[8,128]{1,0:T(8,128)S(1)}) custom-call(s32[8,96]{1,0:T(8,128)S(1)} %copy-done, f32[64,2,18,8,128]{4,3,2,1,0:T(8,128)} %bitcast.26), custom_call_target="tpu_custom_call" | custom-call | flops 99999997952 | bytes 200000000 | tf_op jit(solution)/shard_map/factor_fixed/pallas_call | solution.py:398
  299.4 0.0 all-to-all-done.3
  299.4 0.5 slice.11
  299.9 0.6 reduce_sum.19
  300.5 0.6 broadcast_add_fusion
  301.2 0.0 copy-done.1
  301.2 6.9 %substitute.1 = (f32[1,2048]{1,0:T(1,128)}, f32[1,1024]{1,0:T(1,128)}) custom-call(f32[37,64,8,128]{3,2,1,0:T(8,128)} %get-tuple-element.24.low_ref, f32[8,256,256]{2,1,0:T(8,128)S(1)} %get-tuple-element.25.w_ref, f32[1,2048]{1,0:T(1,128)S(1)} %bitcast.21, bf16[1024,2048]{1,0:T(8,128)(2,1)} %far_ref.1, f32[1,1024]{1,0:T(1,128)S(1)} %copy-done.1), custom_call_target="tpu_custom_call" | custom-call | flops 12000000000 | bytes 24000000 | tf_op jit(solution)/shard_map/substitute/pallas_call | solution.py:539
Async XLA Ops:
  7.2 8.6 %collective-permute-start = (bf16[1024,2048]{1,0:T(8,128)(2,1)}, bf16[1024,2048]{1,0:T(8,128)(2,1)}, u32[]{:S(2)}, u32[]{:S(2)}) collective-permute-start(bf16[1024,2048]{1,0:T(8,128)(2,1)} %far_ref.1), channel_id=1, source_target_pairs={{0,1},{1,0},{2,3},{3,2},{4,5},{5,4},{6,7},{7,6},{8,9},{9,8},{10,11... | collective-permute-start | bytes 12582920 | tf_op jit(solution)/shard_map/ppermute | solution.py:481
  32.2 11.7 %copy-start.4 = (bf16[2048]{0:T(1024)(128)(2,1)S(1)}, bf16[2048]{0:T(1024)(128)(2,1)}, u32[]{:S(2)}) copy-start(bf16[2048]{0:T(1024)(128)(2,1)} %param.10) | copy-start | bytes 12292
  32.2 71.1 %all-to-all-start = ((f32[64,18,8,128]{3,2,1,0:T(8,128)}), f32[64,18,8,128]{3,2,1,0:T(8,128)}, u32[]{:S(2)}, u32[]{:S(2)}) async-start(f32[64,18,8,128]{3,2,1,0:T(8,128)} %gram.1), calls=%async_computation | async-start | bytes 9437184 | tf_op jit(solution)/shard_map/all_to_all | solution.py:487
  43.8 168.2 %all-gather.3.cloned.1.call-start = ((), (), s32[]{:S(2)}) async-start(), calls=%async_computation.4 | async-start | bytes 9510912 | tf_op jit(solution)/shard_map/all_gather | solution.py:501
  55.2 51.3 %copy-start.3 = (bf16[3072,384]{1,0:T(8,128)(2,1)S(1)}, bf16[3072,384]{1,0:T(8,128)(2,1)}, u32[]{:S(2)}) copy-start(bf16[3072,384]{1,0:T(8,128)(2,1)} %get-tuple-element.26) | copy-start | bytes 7077892
  202.2 2.5 copy-start.2
  204.7 7.3 %copy-start = (s32[8,96]{1,0:T(8,128)S(1)}, s32[8,96]{1,0:T(8,128)}, u32[]{:S(2)}) copy-start(s32[8,96]{1,0:T(8,128)} %constant.15.clone.table_ref) | copy-start | bytes 9220
  207.6 91.8 %all-to-all-start.3 = ((f32[128,1,2048]{2,1,0:T(1,128)}), f32[128,1,2048]{2,1,0:T(1,128)S(1)}, u32[]{:S(2)}, u32[]{:S(2)}) async-start(f32[128,1,2048]{2,1,0:T(1,128)} %broadcast_in_dim.2), calls=%async_computation.3 | async-start | bytes 2097152 | tf_op jit(solution)/shard_map/all_to_all | solution.py:532
  212.0 89.2 %copy-start.1 = (f32[1,1024]{1,0:T(1,128)S(1)}, f32[1,1024]{1,0:T(1,128)}, u32[]{:S(2)}) copy-start(f32[1,1024]{1,0:T(1,128)} %get-tuple-element.33.member_ref) | copy-start | bytes 12292
Sparse Core Ops, SparseCore 0:
  106.7 85.9 all-gather.2
